TPU v7x, 32 devices: a whole 2x2x4 slice. The times are simulated.
32 devices in a mesh: space: 4 (over x, core), chan: 8 (over z, y).
Axes of the slice: x: 2, y: 2, z: 4, core: 2. Of those that a mesh axis runs over, the one named last changes fastest.
Arguments:
- inputs: bfloat16 [768, 64, 256], P('chan', 'space'), may hold values from -6 to 6
- initial_state: bfloat16 [384, 64, 256], P('chan', 'space'), may hold values from -6 to 6
- input_weight: bfloat16 [3, 9, 768, 384], P(None, None, 'chan'), may hold values from -0.0625 to 0.0625
- hidden_weight: bfloat16 [3, 9, 384, 384], P(None, None, 'chan'), may hold values from -0.0625 to 0.0625
- gate_bias: float32 [3, 384], replicated, may hold values from -3 to 3
Outputs:
- final_state: bfloat16 [384, 64, 256], P('chan', 'space')
All inputs are finite; a program needn't handle non-finite values.
Results may differ from a plain program's by a relative error of at most 0.0039.
Values may be sent and summed in bfloat16 or wider, within the bound.
A program may use at most 128 MiB of HBM per device.

v0:
```python
import jax
import jax.numpy as jnp
from jax import lax
from jax.sharding import PartitionSpec as P

STEPS = 2
OFFSETS = [(-1, -1), (-1, 0), (-1, 1), (0, -1), (0, 0), (0, 1), (1, -1), (1, 0), (1, 1)]


def extended(value, sides, width):
    for axis, dim in sides:
        count, length = (lax.axis_size(axis), value.shape[dim])
        up = [(i, (i + 1) % count) for i in range(count - 1)]
        down = [(j, i) for i, j in up]
        last = lax.slice_in_dim(value, length - width, length, axis=dim)
        initial = lax.slice_in_dim(value, 0, width, axis=dim)
        before = lax.ppermute(last, axis, up)
        after = lax.ppermute(initial, axis, down)
        value = jnp.concatenate([before, value, after], axis=dim)
    return value


def pad_columns(field):
    return jnp.pad(field, ((0, 0), (0, 0), (1, 1)))


def accumulate(total, padded, weight):
    heights = total.shape[2]
    widths = total.shape[3]
    for tap_index, (row_off, col_off) in enumerate(OFFSETS):
        window = padded[:, 1 + row_off : 1 + row_off + heights, 1 + col_off : 1 + col_off + widths]
        total = total + jnp.einsum(
            "gio,ihw->gohw", weight[:, tap_index], window, preferred_element_type=jnp.float32
        )
    return total


def folder(weight):

    def add_piece(total, piece, start):
        return accumulate(total, piece, weight)

    return add_piece


def per_device(inputs, initial_state, input_weight, hidden_weight, gate_bias):
    own_chan = initial_state.shape[0]
    band_rows = initial_state.shape[1]
    grid_cols = initial_state.shape[2]
    chan_rank = lax.axis_index("chan")
    input_own, hidden_own = (
        lax.all_to_all(input_weight, "chan", split_axis=3, concat_axis=2, tiled=True),
        lax.all_to_all(hidden_weight, "chan", split_axis=3, concat_axis=2, tiled=True),
    )
    input_padded = pad_columns(extended(inputs, (("space", 1),), 1))
    input_empty = jnp.zeros((3, own_chan, band_rows, grid_cols), jnp.float32)
    input_terms = folder(input_own)(
        input_empty, lax.all_gather(input_padded, "chan", axis=0, tiled=True), jnp.int32(0)
    )
    bias_own = lax.dynamic_slice_in_dim(gate_bias, chan_rank * own_chan, own_chan, 1)[
        :, :, None, None
    ]
    gate_fold = folder(hidden_own[0:2])
    cand_fold = folder(hidden_own[2:3])
    current = initial_state
    for repeat in range(STEPS):
        state_padded = pad_columns(extended(current, (("space", 1),), 1))
        gate_empty = jnp.zeros((2, own_chan, band_rows, grid_cols), jnp.float32)
        gate_pre = gate_fold(
            gate_empty, lax.all_gather(state_padded, "chan", axis=0, tiled=True), jnp.int32(0)
        )
        update = jax.nn.sigmoid(input_terms[0] + gate_pre[0] + bias_own[0])
        reset = jax.nn.sigmoid(input_terms[1] + gate_pre[1] + bias_own[1])
        gated = (reset * current.astype(jnp.float32)).astype(jnp.bfloat16)
        gated_padded = pad_columns(extended(gated, (("space", 1),), 1))
        cand_empty = jnp.zeros((1, own_chan, band_rows, grid_cols), jnp.float32)
        cand_pre = cand_fold(
            cand_empty, lax.all_gather(gated_padded, "chan", axis=0, tiled=True), jnp.int32(0)
        )
        candidate = jnp.tanh(input_terms[2] + cand_pre[0] + bias_own[2])
        current = ((1.0 - update) * current.astype(jnp.float32) + update * candidate).astype(
            jnp.bfloat16
        )
    return current


def solution(mesh):
    placed = (
        P("chan", "space", None),
        P("chan", "space", None),
        P(None, None, "chan", None),
        P(None, None, "chan", None),
        P(),
    )
    return jax.shard_map(
        per_device, mesh=mesh, in_specs=placed, out_specs=P("chan", "space", None), check_vma=False
    )
```

profile of v0, /device:TPU:0, one launch (start us, length us, event | category | flops | bytes accessed | tf_op | source)
XLA Modules:
  0.0 706.6 jit_solution(3591301017340858605)
XLA Ops:
  7.7 2.4 collective-permute-start.2
  10.2 1.3 collective-permute-start.3
  11.5 3.9 collective-permute-done.3
  16.9 4.5 collective-permute-start
  21.3 1.3 collective-permute-start.1
  22.7 1.8 collective-permute-done.1
  24.5 1.9 fusion.68
  26.4 4.6 copy.116
  31.0 8.2 %reshape.168 = bf16[8,2,31104]{2,1,0:T(2,128)(2,1)} reshape(bf16[384,3,9,48]{3,2,1,0:T(8,128)(2,1)} %bitcast.410) | data formatting | bytes 1990656
  39.2 5.8 all-to-all-start.1
  45.0 5.2 copy.109
  50.3 37.2 %all-to-all-done.1 = bf16[8,2,31104]{2,1,0:T(2,128)(2,1)S(1)} async-done(((bf16[8,2,31104]{2,1,0:T(2,128)(2,1)}), bf16[8,2,31104]{2,1,0:T(2,128)(2,1)S(1)}, u32[]{:S(2)}, u32[]{:S(2)}) %all-to-all-start.1) | async-done | bytes 995360 | tf_op jit(solution)/shard_map/all_to_all | solution.py:53
  88.5 5.9 all-to-all-start
  94.5 8.1 %reshape.169 = bf16[384,3,9,48]{3,2,1,0:T(8,128)(2,1)} reshape(bf16[8,2,31104]{2,1,0:T(2,128)(2,1)} %copy-done.5) | data formatting | bytes 1990656
  102.6 4.2 copy.182
  106.8 1.5 copy-done.4
  108.3 1.3 slice.435
  109.7 3.6 slice.340
  113.3 121.6 %all-to-all-done = bf16[3,9,96,384]{2,0,1,3:T(4,128)(2,1)S(1)} async-done(((bf16[3,9,96,384]{2,0,1,3:T(4,128)(2,1)}), bf16[3,9,96,384]{2,0,1,3:T(4,128)(2,1)S(1)}, u32[]{:S(2)}, u32[]{:S(2)}) %all-to-all-start) | async-done | bytes 1990688 | tf_op jit(solution)/shard_map/all_to_all | solution.py:52
  236.2 3.3 all_to_all.27
  239.6 4.6 fusion.55
  244.2 2.6 fusion.56
  246.8 1.3 fusion.57
  248.0 1.3 fusion.58
  250.0 1.3 fusion.60
  251.3 1.3 fusion.61
  253.2 3.1 add_bitcast_fusion.2
  256.3 74.9 %all-gather.6.cloned.1.call-done = bf16[768,18,258]{2,0,1:T(8,128)(2,1)} async-done(((bf16[96,18,258]{2,0,1:T(8,128)(2,1)}), bf16[768,18,258]{2,0,1:T(8,128)(2,1)}) %all-gather.6.cloned.1.call-update) | async-done | bytes 7133200 | tf_op jit(solution)/shard_map/all_gather | solution.py:58
  331.2 6.6 fusion.1
  337.8 5.6 fusion.2
  343.4 3.8 fusion.3
  347.2 3.8 fusion.4
  350.9 2.6 fusion.5
  353.5 3.8 fusion.6
  357.3 4.0 fusion.7
  361.2 2.6 fusion.8
  363.8 7.9 %add_bitcast_fusion = f32[3,48,16,256]{3,1,0,2:T(8,128)S(1)} fusion(f32[16,256,3,48]{1,3,2,0:T(8,128)S(1)} %fusion.1, f32[16,256,3,48]{1,3,2,0:T(8,128)} %fusion.2, f32[16,256,3,48]{1,3,2,0:T(8,128)} %fusion.3, f32[16,256,3,48]{1,3,2,0:T(8,128)} %fusion.4, f32[16,256,3,48]{1,3,2,0:T(8,128)} %fusion.5, f32[16,256,3,48]{1,3,2,0:T(8,128)} %fusion.6, ...), kind=kOutput, calls=%fused_computation.94 | convolution fusion | flops 910688256 | bytes 27746304 | tf_op jit(solution)/shard_map/gio,ihw->gohw/dot_general | solution.py:32
  372.1 1.3 collective-permute-start.4
  373.4 1.3 collective-permute-start.5
  374.7 3.5 collective-permute-done.5
  378.2 1.3 fusion.196
  380.8 1.3 slice.368
  382.1 83.5 %all-gather.10.cloned.1.call-done = bf16[384,18,258]{2,0,1:T(8,128)(2,1)} async-done(((bf16[48,18,258]{2,0,1:T(8,128)(2,1)}), bf16[384,18,258]{2,0,1:T(8,128)(2,1)}) %all-gather.10.cloned.1.call-update) | async-done | bytes 3566608 | tf_op jit(solution)/shard_map/all_gather | solution.py:78
  465.6 3.6 fusion.50
  469.2 3.4 fusion.48
  478.9 1.6 fusion.154
  480.5 1.3 collective-permute-start.6
  481.8 1.3 collective-permute-start.7
  483.1 3.5 collective-permute-done.7
  488.0 86.1 %all-gather.12.cloned.1.call-done = bf16[384,18,258]{2,0,1:T(8,128)(2,1)} async-done(((bf16[48,18,258]{2,0,1:T(8,128)(2,1)}), bf16[384,18,258]{2,0,1:T(8,128)(2,1)}) %all-gather.12.cloned.1.call-update) | async-done | bytes 3566608 | tf_op jit(solution)/shard_map/all_gather | solution.py:70
  574.2 3.7 fusion.34
  577.9 2.6 fusion.35
  580.6 1.3 fusion.33
  582.5 1.3 fusion.31
  583.8 1.3 fusion.30
  585.7 1.3 fusion.28
  587.0 1.9 add_bitcast_fusion.1
  590.4 1.3 collective-permute-start.8
  591.7 1.5 collective-permute-start.9
  593.2 3.2 collective-permute-done.9
  597.7 86.4 %all-gather.14.cloned.1.call-done = bf16[384,18,258]{2,0,1:T(8,128)(2,1)} async-done(((bf16[48,18,258]{2,0,1:T(8,128)(2,1)}), bf16[384,18,258]{2,0,1:T(8,128)(2,1)}) %all-gather.14.cloned.1.call-update) | async-done | bytes 3566608 | tf_op jit(solution)/shard_map/all_gather | solution.py:78
  684.1 3.6 fusion.23
  687.7 3.4 fusion.21
  697.3 1.5 fusion.157
  (98 shorter events, 26.8 us)
Async XLA Ops:
  6.5 87.9 %copy-start = (f32[3,384]{1,0:T(4,128)S(1)}, f32[3,384]{1,0:T(4,128)}, u32[]{:S(2)}) copy-start(f32[3,384]{1,0:T(4,128)} %param.9) | copy-start | bytes 13828
  6.5 10.1 %copy-start.20 = (bf16[96,16,256]{2,1,0:T(8,128)(2,1)S(1)}, bf16[96,16,256]{2,1,0:T(8,128)(2,1)}, u32[]{:S(2)}) copy-start(bf16[96,16,256]{2,1,0:T(8,128)(2,1)} %param.5) | copy-start | bytes 2359300
  6.5 233.0 %all-gather.8.cloned.1.call-start = ((), (), s32[]{:S(2)}) async-start(), calls=%async_computation.3 | async-start | bytes 5971968 | tf_op jit(solution)/shard_map/all_gather | solution.py:70
  7.7 3.7 collective-permute-start.2
  10.2 5.2 collective-permute-start.3
  16.5 9.9 %copy-start.17 = (bf16[3,9,48,384]{3,2,1,0:T(8,128)(2,1)S(1)}, bf16[3,9,48,384]{3,2,1,0:T(8,128)(2,1)}, u32[]{:S(2)}) copy-start(bf16[3,9,48,384]{3,2,1,0:T(8,128)(2,1)} %param.8) | copy-start | bytes 2985988
  16.5 314.6 %all-gather.6.cloned.1.call-start = ((), (), s32[]{:S(2)}) async-start(), calls=%async_computation.2 | async-start | bytes 11943936 | tf_op jit(solution)/shard_map/all_gather | solution.py:58
  16.9 5.8 collective-permute-start
  21.3 3.1 collective-permute-start.1
  31.0 14.1 %copy-start.12 = (bf16[3,9,96,384]{3,2,1,0:T(8,128)(2,1)S(1)}, bf16[3,9,96,384]{3,2,1,0:T(8,128)(2,1)}, u32[]{:S(2)}) copy-start(bf16[3,9,96,384]{3,2,1,0:T(8,128)(2,1)} %param.7) | copy-start | bytes 5971972
  39.2 48.3 %all-to-all-start.1 = ((bf16[8,2,31104]{2,1,0:T(2,128)(2,1)}), bf16[8,2,31104]{2,1,0:T(2,128)(2,1)S(1)}, u32[]{:S(2)}, u32[]{:S(2)}) async-start(bf16[8,2,31104]{2,1,0:T(2,128)(2,1)} %reshape.168), calls=%async_computation.1 | async-start | bytes 1990656 | tf_op jit(solution)/shard_map/all_to_all | solution.py:53
  87.5 1.0 copy-start.5
  88.5 146.4 %all-to-all-start = ((bf16[3,9,96,384]{2,0,1,3:T(4,128)(2,1)}), bf16[3,9,96,384]{2,0,1,3:T(4,128)(2,1)S(1)}, u32[]{:S(2)}, u32[]{:S(2)}) async-start(bf16[3,9,96,384]{2,0,1,3:T(4,128)(2,1)} %copy.109), calls=%async_computation | async-start | bytes 7077888 | tf_op jit(solution)/shard_map/all_to_all | solution.py:52
  94.4 371.2 %all-gather.10.cloned.1.call-start = ((), (), s32[]{:S(2)}) async-start(), calls=%async_computation.4 | async-start | bytes 5971968 | tf_op jit(solution)/shard_map/all_gather | solution.py:78
  106.8 1.5 copy-start.4
  236.2 3.4 copy-start.18
  239.6 7.2 %copy-start.13 = (bf16[384,18,258]{2,0,1:T(8,128)(2,1)S(1)}, bf16[384,18,258]{2,0,1:T(8,128)(2,1)}, u32[]{:S(2)}) copy-start(bf16[384,18,258]{2,0,1:T(8,128)(2,1)} %all-gather.8.cloned.1.call-done) | copy-start | bytes 10699780
  253.2 78.0 %copy-start.11 = (bf16[3,9,768,48]{2,3,0,1:T(8,128)(2,1)S(1)}, bf16[3,9,768,48]{2,3,0,1:T(8,128)(2,1)}, u32[]{:S(2)}) copy-start(bf16[3,9,768,48]{2,3,0,1:T(8,128)(2,1)} %all_to_all.27) | copy-start | bytes 5971972
  331.2 12.2 %slice-start = ((s8[10616832]{0:T(1024)(128)(4,1)}), s8[4194304]{0:T(1024)(128)(4,1)S(1)}, s32[]{:S(2)}) async-start(s8[10616832]{0:T(1024)(128)(4,1)} %bitcast.414), calls=%async_computation.7 | async-start | bytes 8388608
  331.2 12.2 %slice-start.1 = ((s8[10616832]{0:T(1024)(128)(4,1)}), s8[4194304]{0:T(1024)(128)(4,1)S(1)}, s32[]{:S(2)}) async-start(s8[10616832]{0:T(1024)(128)(4,1)} %bitcast.414), calls=%async_computation.8 | async-start | bytes 8388608
  337.8 5.6 slice-start.2
  363.8 7.9 %copy-start.6 = (f32[2,48,16,256]{3,1,2,0:T(8,128)S(1)}, f32[2,48,16,256]{3,1,2,0:T(8,128)}, u32[]{:S(2)}) copy-start(f32[2,48,16,256]{3,1,2,0:T(8,128)} %add_bitcast_fusion.2) | copy-start | bytes 4718596
  363.8 7.9 %copy-start.15 = (bf16[48,16,256]{2,1,0:T(8,128)(2,1)S(1)}, bf16[48,16,256]{2,1,0:T(8,128)(2,1)}, u32[]{:S(2)}) copy-start(bf16[48,16,256]{2,1,0:T(8,128)(2,1)} %param.6) | copy-start | bytes 1179652
  372.1 2.6 collective-permute-start.4
  373.4 4.8 collective-permute-start.5
  379.5 194.7 %all-gather.12.cloned.1.call-start = ((), (), s32[]{:S(2)}) async-start(), calls=%async_computation.5 | async-start | bytes 5971968 | tf_op jit(solution)/shard_map/all_gather | solution.py:70
  382.1 87.1 %copy-start.10 = (bf16[1,9,384,48]{2,3,1,0:T(8,128)(2,1)S(1)}, bf16[1,9,384,48]{2,3,1,0:T(8,128)(2,1)}, u32[]{:S(2)}) copy-start(bf16[1,9,384,48]{2,3,1,0:T(8,128)(2,1)} %slice.368) | copy-start | bytes 995332
  465.6 7.1 %copy-start.2 = (bf16[384,18,258]{2,0,1:T(8,128)(2,1)S(1)}, bf16[384,18,258]{2,0,1:T(8,128)(2,1)}, u32[]{:S(2)}) copy-start(bf16[384,18,258]{2,0,1:T(8,128)(2,1)} %all-gather.10.cloned.1.call-done) | copy-start | bytes 10699780
  477.4 1.4 copy-start.7
  477.4 1.5 copy-start.16
  480.5 2.6 collective-permute-start.6
  481.8 4.8 collective-permute-start.7
  487.8 196.3 %all-gather.14.cloned.1.call-start = ((), (), s32[]{:S(2)}) async-start(), calls=%async_computation.6 | async-start | bytes 5971968 | tf_op jit(solution)/shard_map/all_gather | solution.py:78
  574.2 6.4 copy-start.14
  577.9 2.7 copy-start.19
  588.9 1.2 copy-start.8
  590.4 2.9 collective-permute-start.8
  591.7 4.8 collective-permute-start.9
  684.1 7.1 copy-start.3
  695.8 1.4 copy-start.9
  695.9 3.8 copy-start.1
Sparse Core Ops, SparseCore 0:
  16.7 123.2 all-gather.7
  142.2 188.9 all-gather.5
  379.6 85.9 all-gather.9
  487.9 86.2 all-gather.11
  597.8 86.2 all-gather.13
where the time goes:
time: 714 us; the launch traced here: 707 us
  waiting for transfers between devices  506 us (71%)
  matrix products  99.9 us (14%)
  local copies, waits for them, and re-layouts  49.9 us (7%)
  starting transfers between devices  29.6 us (4%)
  between operations  14.2 us (2%)
  other arithmetic  7.41 us (1%)
    all_gather x2, waiting for transfers between devices, per_device(): lax.all_gather(gated_padded, 'chan', axis=0, tiled=True)  170 us
    all_to_all x1, waiting for transfers between devices, per_device(): lax.all_to_all(input_weight, 'chan', split_axis=3, concat_axis=2, tiled=T...  122 us
    dot_general x45, matrix products, accumulate(): jnp.einsum('gio,ihw->gohw', weight[:, tap_index], window, preferred_eleme...  99.9 us
    all_gather x2, waiting for transfers between devices, per_device(): lax.all_gather(state_padded, 'chan', axis=0, tiled=True)  86.1 us
    all_gather x1, waiting for transfers between devices, per_device(): lax.all_gather(input_padded, 'chan', axis=0, tiled=True)  74.9 us
    all_to_all x1, waiting for transfers between devices, per_device(): lax.all_to_all(hidden_weight, 'chan', split_axis=3, concat_axis=2, tiled=...  37.2 us
    unnamed x54, local copies, waits for them, and re-layouts  32.5 us
    ppermute x5, waiting for transfers between devices, extended(): after = lax.ppermute(initial, axis, down)  15.9 us
  transfers between devices with their start and end apart: 17, of which 11 were waited for; matrix products, arithmetic and copies ran while one was open for 8% of the time, Pallas kernels for 0%

commit v1 on v0

--- a/solution.py
+++ b/solution.py
@@ -5,6 +5,13 @@
 
 STEPS = 2
 OFFSETS = [(-1, -1), (-1, 0), (-1, 1), (0, -1), (0, 0), (0, 1), (1, -1), (1, 0), (1, 1)]
+
+
+def swapped_in(block, name, along):
+    size = lax.axis_size(name)
+    blocks = jnp.stack([block for _ in range(size)])
+    blocks = lax.all_to_all(blocks, name, split_axis=0, concat_axis=0)
+    return jnp.concatenate(blocks, axis=along)
 
 
 def extended(value, sides, width):
@@ -74,9 +81,7 @@
         gated = (reset * current.astype(jnp.float32)).astype(jnp.bfloat16)
         gated_padded = pad_columns(extended(gated, (("space", 1),), 1))
         cand_empty = jnp.zeros((1, own_chan, band_rows, grid_cols), jnp.float32)
-        cand_pre = cand_fold(
-            cand_empty, lax.all_gather(gated_padded, "chan", axis=0, tiled=True), jnp.int32(0)
-        )
+        cand_pre = cand_fold(cand_empty, swapped_in(gated_padded, "chan", 0), jnp.int32(0))
         candidate = jnp.tanh(input_terms[2] + cand_pre[0] + bias_own[2])
         current = ((1.0 - update) * current.astype(jnp.float32) + update * candidate).astype(
             jnp.bfloat16

time: 714 us -> 779 us (1.091)
  blocking collectives: 0 us -> 121 us
  waiting for transfers between devices: 506 us -> 449 us
  matrix products: 99.9 us -> 89.7 us
    all_gather x2 -> x0, waiting for transfers between devices: 170 us -> none  [per_device(): lax.all_gather(gated_padded, 'chan', axis=0, tiled=True)]
    all_to_all x0 -> x1, blocking collectives: none -> 121 us  [swapped_in(): blocks = lax.all_to_all(blocks, name, split_axis=0, concat_axis=0)]
    all_to_all x0 -> x1, waiting for transfers between devices: none -> 115 us  [swapped_in(): blocks = lax.all_to_all(blocks, name, split_axis=0, concat_axis=0)]
    dot_general x45, matrix products: 99.9 us -> 89.7 us  [accumulate(): jnp.einsum('gio,ihw->gohw', weight[:, tap_index], window, preferred_eleme...]
    unnamed x54 -> x46, local copies, waits for them, and re-layouts: 32.5 us -> 30.8 us
  transfers between devices with their start and end apart: 17 -> 16, of which waited for: 11 -> 10; matrix products, arithmetic and copies ran while one was open for 8% -> 7% of each run, Pallas kernels for 0% -> 0%
where the time goes in v1:
time: 779 us; the launch traced here: 771 us
  waiting for transfers between devices  449 us (58%)
  blocking collectives  121 us (16%)
  matrix products  89.7 us (12%)
  local copies, waits for them, and re-layouts  55.7 us (7%)
  starting transfers between devices  35.9 us (5%)
  between operations  14.2 us (2%)
    all_to_all x1, waiting for transfers between devices, per_device(): lax.all_to_all(input_weight, 'chan', split_axis=3, concat_axis=2, tiled=T...  122 us
    all_to_all x1, blocking collectives, swapped_in(): blocks = lax.all_to_all(blocks, name, split_axis=0, concat_axis=0)  121 us
    all_to_all x1, waiting for transfers between devices, swapped_in(): blocks = lax.all_to_all(blocks, name, split_axis=0, concat_axis=0)  115 us
    dot_general x45, matrix products, accumulate(): jnp.einsum('gio,ihw->gohw', weight[:, tap_index], window, preferred_eleme...  89.7 us
    all_gather x2, waiting for transfers between devices, per_device(): lax.all_gather(state_padded, 'chan', axis=0, tiled=True)  86.3 us
    all_gather x1, waiting for transfers between devices, per_device(): lax.all_gather(input_padded, 'chan', axis=0, tiled=True)  74.3 us
    all_to_all x1, waiting for transfers between devices, per_device(): lax.all_to_all(hidden_weight, 'chan', split_axis=3, concat_axis=2, tiled=...  37.2 us
    unnamed x46, local copies, waits for them, and re-layouts  30.8 us
  transfers between devices with their start and end apart: 16, of which 10 were waited for; matrix products, arithmetic and copies ran while one was open for 7% of the time, Pallas kernels for 0%

profile of v1, /device:TPU:0, one launch (start us, length us, event | category | flops | bytes accessed | tf_op | source)
XLA Modules:
  0.0 771.2 jit_solution(15794956840456651753)
XLA Ops:
  6.5 1.2 copy.115
  7.7 2.4 collective-permute-start.2
  10.2 1.3 collective-permute-start.3
  11.5 3.9 collective-permute-done.3
  15.3 1.2 fusion.194
  16.9 4.5 collective-permute-start
  21.3 1.3 collective-permute-start.1
  22.6 1.8 collective-permute-done.1
  24.5 1.9 fusion.68
  26.4 4.6 copy.118
  31.0 8.2 %reshape.180 = bf16[8,2,31104]{2,1,0:T(2,128)(2,1)} reshape(bf16[384,3,9,48]{3,2,1,0:T(8,128)(2,1)} %bitcast.430) | data formatting | bytes 1990656
  39.2 5.8 all-to-all-start.1
  45.1 5.2 copy.111
  50.3 37.2 %all-to-all-done.1 = bf16[8,2,31104]{2,1,0:T(2,128)(2,1)S(1)} async-done(((bf16[8,2,31104]{2,1,0:T(2,128)(2,1)}), bf16[8,2,31104]{2,1,0:T(2,128)(2,1)S(1)}, u32[]{:S(2)}, u32[]{:S(2)}) %all-to-all-start.1) | async-done | bytes 995360 | tf_op jit(solution)/shard_map/all_to_all | solution.py:60
  88.5 5.9 all-to-all-start
  94.5 8.1 %reshape.181 = bf16[384,3,9,48]{3,2,1,0:T(8,128)(2,1)} reshape(bf16[8,2,31104]{2,1,0:T(2,128)(2,1)} %copy-done.3) | data formatting | bytes 1990656
  102.6 4.2 copy.186
  106.8 1.5 copy-done.2
  108.3 1.3 slice.435
  109.6 3.6 slice.340
  113.3 122.4 %all-to-all-done = bf16[3,9,96,384]{2,0,1,3:T(4,128)(2,1)S(1)} async-done(((bf16[3,9,96,384]{2,0,1,3:T(4,128)(2,1)}), bf16[3,9,96,384]{2,0,1,3:T(4,128)(2,1)S(1)}, u32[]{:S(2)}, u32[]{:S(2)}) %all-to-all-start) | async-done | bytes 1990688 | tf_op jit(solution)/shard_map/all_to_all | solution.py:59
  237.0 3.3 all_to_all.33
  240.4 4.3 fusion.55
  244.7 2.6 fusion.56
  247.3 1.3 fusion.57
  248.5 1.3 fusion.58
  250.5 1.3 fusion.60
  251.8 1.3 fusion.61
  253.7 3.0 add_bitcast_fusion.2
  256.8 74.3 %all-gather.4.cloned.1.call-done = bf16[768,18,258]{2,0,1:T(8,128)(2,1)} async-done(((bf16[96,18,258]{2,0,1:T(8,128)(2,1)}), bf16[768,18,258]{2,0,1:T(8,128)(2,1)}) %all-gather.4.cloned.1.call-update) | async-done | bytes 7133200 | tf_op jit(solution)/shard_map/all_gather | solution.py:65
  331.1 6.6 fusion.1
  337.7 5.6 fusion.2
  343.3 3.8 fusion.3
  347.1 3.8 fusion.4
  350.9 2.5 fusion.5
  353.4 3.7 fusion.6
  357.1 3.9 fusion.7
  361.1 2.6 fusion.8
  363.7 7.9 %add_bitcast_fusion = f32[3,48,16,256]{3,1,0,2:T(8,128)S(1)} fusion(f32[16,256,3,48]{1,3,2,0:T(8,128)S(1)} %fusion.1, f32[16,256,3,48]{1,3,2,0:T(8,128)} %fusion.2, f32[16,256,3,48]{1,3,2,0:T(8,128)} %fusion.3, f32[16,256,3,48]{1,3,2,0:T(8,128)} %fusion.4, f32[16,256,3,48]{1,3,2,0:T(8,128)} %fusion.5, f32[16,256,3,48]{1,3,2,0:T(8,128)} %fusion.6, ...), kind=kOutput, calls=%fused_computation.94 | convolution fusion | flops 910688256 | bytes 27746304 | tf_op jit(solution)/shard_map/gio,ihw->gohw/dot_general | solution.py:39
  372.0 1.3 collective-permute-start.4
  373.3 1.3 collective-permute-start.5
  374.6 3.5 collective-permute-done.5
  378.4 2.9 stack.4
  381.3 4.7 all-to-all-start.2
  386.0 1.2 slice.455
  387.2 1.3 slice.368
  388.6 114.7 %all-to-all-done.2 = bf16[8,48,18,258]{3,1,2,0:T(8,128)(2,1)} async-done(((bf16[8,48,18,258]{3,1,2,0:T(8,128)(2,1)}), bf16[8,48,18,258]{3,1,2,0:T(8,128)(2,1)}, u32[]{:S(2)}, u32[]{:S(2)}) %all-to-all-start.2) | async-done | bytes 3566624 | tf_op jit(solution)/shard_map/all_to_all | solution.py:13
  503.3 3.3 copy.132
  516.5 3.3 collective-permute-start.6
  519.8 1.5 collective-permute-start.7
  521.3 1.6 collective-permute-done.7
  522.9 1.2 select_maximum_fusion.2
  524.1 86.2 %all-gather.8.cloned.1.call-done = bf16[384,18,258]{2,0,1:T(8,128)(2,1)} async-done(((bf16[48,18,258]{2,0,1:T(8,128)(2,1)}), bf16[384,18,258]{2,0,1:T(8,128)(2,1)}) %all-gather.8.cloned.1.call-update) | async-done | bytes 3566608 | tf_op jit(solution)/shard_map/all_gather | solution.py:77
  610.3 3.7 fusion.34
  614.1 2.6 fusion.35
  616.7 1.3 fusion.33
  618.7 1.3 fusion.31
  620.0 1.3 fusion.30
  622.0 1.3 fusion.28
  623.4 1.9 add_bitcast_fusion.1
  625.6 1.3 collective-permute-start.8
  626.9 1.3 collective-permute-start.9
  628.2 3.5 collective-permute-done.9
  632.5 120.9 %all_to_all.43 = bf16[8,48,18,258]{3,1,2,0:T(8,128)(2,1)S(1)} all-to-all(bf16[8,48,18,258]{3,1,2,0:T(8,128)(2,1)S(1)} %stack.5), channel_id=1, replica_groups=mesh['space'=4,'chan'=8] {'chan'}, dimensions={0} | all-to-all | bytes 7133184 | tf_op jit(solution)/shard_map/all_to_all | solution.py:13
  (91 shorter events, 27.9 us)
Async XLA Ops:
  6.5 87.9 %copy-start = (f32[3,384]{1,0:T(4,128)S(1)}, f32[3,384]{1,0:T(4,128)}, u32[]{:S(2)}) copy-start(f32[3,384]{1,0:T(4,128)} %param.9) | copy-start | bytes 13828
  6.5 10.0 %copy-start.16 = (bf16[96,16,256]{2,1,0:T(8,128)(2,1)S(1)}, bf16[96,16,256]{2,1,0:T(8,128)(2,1)}, u32[]{:S(2)}) copy-start(bf16[96,16,256]{2,1,0:T(8,128)(2,1)} %param.5) | copy-start | bytes 2359300
  6.5 233.9 %all-gather.6.cloned.1.call-start = ((), (), s32[]{:S(2)}) async-start(), calls=%async_computation.5 | async-start | bytes 5971968 | tf_op jit(solution)/shard_map/all_gather | solution.py:77
  7.7 3.7 collective-permute-start.2
  10.2 5.2 collective-permute-start.3
  16.5 9.9 %copy-start.13 = (bf16[3,9,48,384]{3,2,1,0:T(8,128)(2,1)S(1)}, bf16[3,9,48,384]{3,2,1,0:T(8,128)(2,1)}, u32[]{:S(2)}) copy-start(bf16[3,9,48,384]{3,2,1,0:T(8,128)(2,1)} %param.8) | copy-start | bytes 2985988
  16.5 314.5 %all-gather.4.cloned.1.call-start = ((), (), s32[]{:S(2)}) async-start(), calls=%async_computation.4 | async-start | bytes 11943936 | tf_op jit(solution)/shard_map/all_gather | solution.py:65
  16.9 5.8 collective-permute-start
  21.3 3.1 collective-permute-start.1
  31.0 14.1 %copy-start.8 = (bf16[3,9,96,384]{3,2,1,0:T(8,128)(2,1)S(1)}, bf16[3,9,96,384]{3,2,1,0:T(8,128)(2,1)}, u32[]{:S(2)}) copy-start(bf16[3,9,96,384]{3,2,1,0:T(8,128)(2,1)} %param.7) | copy-start | bytes 5971972
  39.2 48.3 %all-to-all-start.1 = ((bf16[8,2,31104]{2,1,0:T(2,128)(2,1)}), bf16[8,2,31104]{2,1,0:T(2,128)(2,1)S(1)}, u32[]{:S(2)}, u32[]{:S(2)}) async-start(bf16[8,2,31104]{2,1,0:T(2,128)(2,1)} %reshape.180), calls=%async_computation.1 | async-start | bytes 1990656 | tf_op jit(solution)/shard_map/all_to_all | solution.py:60
  87.5 1.0 copy-start.3
  88.5 147.2 %all-to-all-start = ((bf16[3,9,96,384]{2,0,1,3:T(4,128)(2,1)}), bf16[3,9,96,384]{2,0,1,3:T(4,128)(2,1)S(1)}, u32[]{:S(2)}, u32[]{:S(2)}) async-start(bf16[3,9,96,384]{2,0,1,3:T(4,128)(2,1)} %copy.111), calls=%async_computation | async-start | bytes 7077888 | tf_op jit(solution)/shard_map/all_to_all | solution.py:59
  106.8 1.5 copy-start.2
  237.0 3.4 copy-start.14
  240.4 6.8 copy-start.9
  253.7 77.4 %copy-start.7 = (bf16[3,9,768,48]{2,3,0,1:T(8,128)(2,1)S(1)}, bf16[3,9,768,48]{2,3,0,1:T(8,128)(2,1)}, u32[]{:S(2)}) copy-start(bf16[3,9,768,48]{2,3,0,1:T(8,128)(2,1)} %all_to_all.33) | copy-start | bytes 5971972
  331.1 12.2 %slice-start = ((s8[10616832]{0:T(1024)(128)(4,1)}), s8[4194304]{0:T(1024)(128)(4,1)S(1)}, s32[]{:S(2)}) async-start(s8[10616832]{0:T(1024)(128)(4,1)} %bitcast.434), calls=%async_computation.7 | async-start | bytes 8388608
  331.1 12.2 %slice-start.1 = ((s8[10616832]{0:T(1024)(128)(4,1)}), s8[4194304]{0:T(1024)(128)(4,1)S(1)}, s32[]{:S(2)}) async-start(s8[10616832]{0:T(1024)(128)(4,1)} %bitcast.434), calls=%async_computation.8 | async-start | bytes 8388608
  337.7 5.6 slice-start.2
  363.7 7.9 %copy-start.4 = (f32[2,48,16,256]{3,1,2,0:T(8,128)S(1)}, f32[2,48,16,256]{3,1,2,0:T(8,128)}, u32[]{:S(2)}) copy-start(f32[2,48,16,256]{3,1,2,0:T(8,128)} %add_bitcast_fusion.2) | copy-start | bytes 4718596
  363.7 7.9 %copy-start.11 = (bf16[48,16,256]{2,1,0:T(8,128)(2,1)S(1)}, bf16[48,16,256]{2,1,0:T(8,128)(2,1)}, u32[]{:S(2)}) copy-start(bf16[48,16,256]{2,1,0:T(8,128)(2,1)} %param.6) | copy-start | bytes 1179652
  372.0 2.6 collective-permute-start.4
  373.3 4.8 collective-permute-start.5
  381.3 122.0 %all-to-all-start.2 = ((bf16[8,48,18,258]{3,1,2,0:T(8,128)(2,1)}), bf16[8,48,18,258]{3,1,2,0:T(8,128)(2,1)}, u32[]{:S(2)}, u32[]{:S(2)}) async-start(bf16[8,48,18,258]{3,1,2,0:T(8,128)(2,1)} %stack.4), calls=%async_computation.2 | async-start | bytes 10616832 | tf_op jit(solution)/shard_map/all_to_all | solution.py:13
  386.0 224.4 %all-gather.8.cloned.1.call-start = ((), (), s32[]{:S(2)}) async-start(), calls=%async_computation.6 | async-start | bytes 5971968 | tf_op jit(solution)/shard_map/all_gather | solution.py:77
  388.6 118.1 %copy-start.6 = (bf16[1,9,384,48]{2,3,1,0:T(8,128)(2,1)S(1)}, bf16[1,9,384,48]{2,3,1,0:T(8,128)(2,1)}, u32[]{:S(2)}) copy-start(bf16[1,9,384,48]{2,3,1,0:T(8,128)(2,1)} %slice.368) | copy-start | bytes 995332
  514.0 1.4 copy-start.5
  514.0 1.5 copy-start.12
  516.5 4.8 collective-permute-start.6
  519.8 3.1 collective-permute-start.7
  610.3 6.4 copy-start.10
  614.1 2.7 copy-start.15
  625.6 2.6 collective-permute-start.8
  626.9 4.8 collective-permute-start.9
  761.6 2.6 copy-start.1
Sparse Core Ops, SparseCore 0:
  16.7 123.0 all-gather.5
  141.9 189.0 all-gather.3
  524.2 86.0 all-gather.7
